TPU v7x, 32 devices: a whole 2x2x4 slice. The times are simulated.
32 devices in a mesh: agent: 8 (over y, x, core), res: 4 (over z).
Axes of the slice: x: 2, y: 2, z: 4, core: 2. Of those that a mesh axis runs over, the one named last changes fastest.
Arguments:
- linear_cost: float32 [2048, 2048], P('agent', 'res'), may hold values from -6 to 6
- agent_type: int32 [2048], P('agent'), may hold values from 0 to 3, as said below
- block_mask: int32 [2048, 16], P('agent', 'res'), may hold values 0 or 1
- inverses: bfloat16 [4, 2048, 2048], P(None, 'res'), as said below
- cost_weight: float32 [2048], P('res'), may hold values from 0.5 to 8
- target: float32 [2048], P('res'), may hold values from -6 to 6
Outputs:
- usage: float32 [2048, 2048], P('agent', 'res')
- shared: float32 [2048], P('res')
- prices: float32 [2048], P('res')
- primal_norm: float32 [5], replicated
- dual_norm: float32 [5], replicated
Inputs may be any that keep to these rules, and one draw needn't show every extreme that they name: Each inverses[k] is exactly symmetric: inverses[k, i, j] equals inverses[k, j, i]. `agent_type`: each aligned block of 256 agents (the agents held by one device along the agent axis) holds exactly 64 agents of each type, in no particular order.
All inputs are finite; a program needn't handle non-finite values. No bound on the sum of `block_mask` on one device may be relied on, other than what follows from the above.
Results may differ from a plain program's by a relative error of at most 0.0039.
Values may be sent and summed in bfloat16 or wider, within the bound.
No kernel may reach another device: no remote copies, remote signals or barrier semaphores. Data moves between devices by JAX's collectives and lax.ppermute only.
A program may use at most 64 MiB of HBM per device.

v0:
```python
import jax
import jax.numpy as jnp
from jax import lax
from jax.sharding import PartitionSpec as P

BLK = 128
ITERS = 5
penalty = 1.0
eps = 1e-06


def on_device(linear_cost, agent_type, block_mask, inverses, cost_weight, target):
    local_agents, local_width = linear_cost.shape
    type_count = inverses.shape[0]
    group_rows = local_agents // type_count
    count = local_agents * lax.axis_size("agent")
    block_count = block_mask.shape[1]
    order = jnp.argsort(agent_type, stable=True)
    restore = jnp.argsort(order, stable=True)
    expand = jnp.broadcast_to(
        block_mask.astype(jnp.float32)[:, :, None], (local_agents, block_count, BLK)
    ).reshape(local_agents, local_width)
    usage = jnp.zeros(linear_cost.shape, jnp.float32)
    mean_usage = jnp.zeros((local_width,), jnp.float32)
    shared = jnp.zeros((local_width,), jnp.float32)
    prices = jnp.zeros((local_width,), jnp.float32)
    primal_list = []
    dual_list = []
    for iteration in range(ITERS):
        rhs = (penalty * (usage - mean_usage + shared - prices) - linear_cost).astype(jnp.bfloat16)
        grouped = rhs[order].reshape(type_count, group_rows, local_width)
        product = jnp.einsum(
            "tas,tws->taw",
            lax.all_gather(grouped, "res", axis=2, tiled=True),
            inverses,
            preferred_element_type=jnp.float32,
        )
        new_usage = product.reshape(local_agents, local_width)[restore]
        new_usage = new_usage * expand
        change_local = penalty * penalty * jnp.sum((new_usage - usage) ** 2)
        usage = new_usage
        column_sum = jnp.sum(usage, axis=0)
        usage_sum = lax.psum(column_sum, "agent")
        dual2 = lax.psum(change_local, ("agent", "res"))
        mean_usage = usage_sum / count
        shared = (cost_weight * target + penalty * (prices + mean_usage)) / (cost_weight + penalty)
        prices = prices + mean_usage - shared
        primal2 = lax.psum(count * jnp.sum((mean_usage - shared) ** 2), "res")
        primal_list.append(jnp.sqrt(primal2 + eps))
        dual_list.append(jnp.sqrt(dual2 + eps))
    primal_norm = jnp.stack(primal_list)
    dual_norm = jnp.stack(dual_list)
    return (usage, shared, prices, primal_norm, dual_norm)


def solution(mesh):
    placed = (
        P("agent", "res"),
        P("agent"),
        P("agent", "res"),
        P(None, "res", None),
        P("res"),
        P("res"),
    )
    return jax.shard_map(
        on_device,
        mesh=mesh,
        in_specs=placed,
        out_specs=(P("agent", "res"), P("res"), P("res"), P(), P()),
        check_vma=False,
    )
```

profile of v0, /device:TPU:12, one launch (start us, length us, event | category | flops | bytes accessed | tf_op | source)
XLA Modules:
  0.0 334.9 jit_solution(6932095263842248031)
XLA Ops:
  7.2 0.0 all-gather.6.cloned.1.call-start
  7.2 3.8 %sort.31 = (s32[256]{0:T(256)}, s32[256]{0:T(256)S(1)}) sort(s32[256]{0:T(256)} %param.7, s32[256]{0:T(256)S(1)} %iota.7), dimensions={0}, to_apply=%region_0.0 | sort | flops 2048 | bytes 4096 | tf_op jit(solution)/shard_map/jit(argsort)/sort | solution.py:18
  11.1 1.1 subtract_convert_fusion.4
  12.2 1.9 gather_fusion
  14.0 0.0 all-gather.6.cloned.1.call-update
  14.0 0.0 all-gather.8.cloned.1.call-start
  14.1 3.2 sort.32
  17.3 0.7 convert_element_type.19
  18.0 0.1 copy.11
  18.1 0.0 copy-start.1
  18.1 0.0 copy-start.3
  18.1 0.0 copy-start
  18.2 25.1 %all-gather.6.cloned.1.call-done = bf16[4,64,2048]{2,1,0:T(8,128)(2,1)} async-done(((bf16[4,64,512]{2,1,0:T(8,128)(2,1)}), bf16[4,64,2048]{2,1,0:T(8,128)(2,1)}) %all-gather.6.cloned.1.call-update) | async-done | bytes 1048592 | tf_op jit(solution)/shard_map/all_gather | solution.py:34
  43.3 6.4 %fusion.13 = f32[4,64,512]{2,1,0:T(8,128)S(1)} fusion(bf16[4,64,2048]{2,1,0:T(8,128)(2,1)} %all-gather.6.cloned.1.call-done, bf16[4,512,2048]{2,1,0:T(8,128)(2,1)} %param.9), kind=kOutput, calls=%fused_computation.56 | convolution fusion | flops 536870912 | bytes 9961472 | tf_op jit(solution)/shard_map/tas,tws->taw/dot_general | solution.py:32
  49.7 1.0 gather_fusion.1
  50.7 0.3 broadcast_in_dim.11
  51.0 0.1 fusion.12
  51.1 11.9 %psum.105 = f32[512]{0:T(512)S(1)} all-reduce(f32[512]{0:T(512)S(1)} %get-tuple-element.44), channel_id=1, replica_groups=mesh['agent'=8,'res'=4] {'agent'}, use_global_device_ids=true, to_apply=%region_3.4 | all-reduce | flops 512 | bytes 4096 | tf_op jit(solution)/shard_map/psum | solution.py:43
  63.0 0.0 copy-done.3
  63.0 0.6 multiply_reduce_fusion.9
  63.6 0.1 subtract_convert_fusion.3
  63.7 1.9 gather_fusion.2
  65.6 0.0 all-gather.8.cloned.1.call-update
  65.6 0.0 all-gather.10.cloned.1.call-start
  65.7 27.5 %all-gather.8.cloned.1.call-done = bf16[4,64,2048]{2,1,0:T(8,128)(2,1)} async-done(((bf16[4,64,512]{2,1,0:T(8,128)(2,1)}), bf16[4,64,2048]{2,1,0:T(8,128)(2,1)}) %all-gather.8.cloned.1.call-update) | async-done | bytes 1048592 | tf_op jit(solution)/shard_map/all_gather | solution.py:34
  93.1 6.4 %fusion.14 = f32[4,64,512]{2,1,0:T(8,128)S(1)} fusion(bf16[4,64,2048]{2,1,0:T(8,128)(2,1)} %all-gather.8.cloned.1.call-done, bf16[4,512,2048]{2,1,0:T(8,128)(2,1)} %param.9), kind=kOutput, calls=%fused_computation.57 | convolution fusion | flops 536870912 | bytes 9961472 | tf_op jit(solution)/shard_map/tas,tws->taw/dot_general | solution.py:32
  99.5 1.0 gather_fusion.3
  100.5 0.1 fusion.11
  100.6 11.9 %psum.106 = f32[512]{0:T(512)S(1)} all-reduce(f32[512]{0:T(512)S(1)} %get-tuple-element.42), channel_id=1, replica_groups=mesh['agent'=8,'res'=4] {'agent'}, use_global_device_ids=true, to_apply=%region_5.6 | all-reduce | flops 512 | bytes 4096 | tf_op jit(solution)/shard_map/psum | solution.py:43
  112.5 0.6 multiply_reduce_fusion.8
  113.1 0.1 subtract_convert_fusion.2
  113.2 1.9 gather_fusion.4
  115.0 0.0 all-gather.10.cloned.1.call-update
  115.1 0.0 all-gather.12.cloned.1.call-start
  115.1 27.5 %all-gather.10.cloned.1.call-done = bf16[4,64,2048]{2,1,0:T(8,128)(2,1)} async-done(((bf16[4,64,512]{2,1,0:T(8,128)(2,1)}), bf16[4,64,2048]{2,1,0:T(8,128)(2,1)}) %all-gather.10.cloned.1.call-update) | async-done | bytes 1048592 | tf_op jit(solution)/shard_map/all_gather | solution.py:34
  142.6 6.4 %fusion.15 = f32[4,64,512]{2,1,0:T(8,128)S(1)} fusion(bf16[4,64,2048]{2,1,0:T(8,128)(2,1)} %all-gather.10.cloned.1.call-done, bf16[4,512,2048]{2,1,0:T(8,128)(2,1)} %param.9), kind=kOutput, calls=%fused_computation.58 | convolution fusion | flops 536870912 | bytes 9961472 | tf_op jit(solution)/shard_map/tas,tws->taw/dot_general | solution.py:32
  148.9 1.0 gather_fusion.5
  149.9 0.1 fusion.10
  150.0 12.1 %psum.107 = f32[512]{0:T(512)S(1)} all-reduce(f32[512]{0:T(512)S(1)} %get-tuple-element.40), channel_id=1, replica_groups=mesh['agent'=8,'res'=4] {'agent'}, use_global_device_ids=true, to_apply=%region_7.8 | all-reduce | flops 512 | bytes 4096 | tf_op jit(solution)/shard_map/psum | solution.py:43
  162.1 0.6 multiply_reduce_fusion.7
  162.7 0.1 subtract_convert_fusion.1
  162.8 1.9 gather_fusion.6
  164.7 0.0 all-gather.12.cloned.1.call-update
  164.7 0.0 all-gather.14.cloned.1.call-start
  164.8 27.4 %all-gather.12.cloned.1.call-done = bf16[4,64,2048]{2,1,0:T(8,128)(2,1)} async-done(((bf16[4,64,512]{2,1,0:T(8,128)(2,1)}), bf16[4,64,2048]{2,1,0:T(8,128)(2,1)}) %all-gather.12.cloned.1.call-update) | async-done | bytes 1048592 | tf_op jit(solution)/shard_map/all_gather | solution.py:34
  192.2 6.4 %fusion.16 = f32[4,64,512]{2,1,0:T(8,128)S(1)} fusion(bf16[4,64,2048]{2,1,0:T(8,128)(2,1)} %all-gather.12.cloned.1.call-done, bf16[4,512,2048]{2,1,0:T(8,128)(2,1)} %param.9), kind=kOutput, calls=%fused_computation.59 | convolution fusion | flops 536870912 | bytes 9961472 | tf_op jit(solution)/shard_map/tas,tws->taw/dot_general | solution.py:32
  198.6 1.8 gather_fusion.7
  200.4 1.2 fusion.9
  201.5 11.9 %psum.108 = f32[512]{0:T(512)S(1)} all-reduce(f32[512]{0:T(512)S(1)} %get-tuple-element.38), channel_id=1, replica_groups=mesh['agent'=8,'res'=4] {'agent'}, use_global_device_ids=true, to_apply=%region_9.10 | all-reduce | flops 512 | bytes 4096 | tf_op jit(solution)/shard_map/psum | solution.py:43
  213.4 0.6 multiply_reduce_fusion.6
  214.0 0.1 subtract_convert_fusion
  214.1 1.9 gather_fusion.8
  216.0 0.0 all-gather.14.cloned.1.call-update
  218.6 24.9 %all-gather.14.cloned.1.call-done = bf16[4,64,2048]{2,1,0:T(8,128)(2,1)} async-done(((bf16[4,64,512]{2,1,0:T(8,128)(2,1)}), bf16[4,64,2048]{2,1,0:T(8,128)(2,1)}) %all-gather.14.cloned.1.call-update) | async-done | bytes 1048592 | tf_op jit(solution)/shard_map/all_gather | solution.py:34
  243.5 6.4 %fusion.17 = f32[4,64,512]{2,1,0:T(8,128)S(1)} fusion(bf16[4,64,2048]{2,1,0:T(8,128)(2,1)} %all-gather.14.cloned.1.call-done, bf16[4,512,2048]{2,1,0:T(8,128)(2,1)} %param.9), kind=kOutput, calls=%fused_computation.60 | convolution fusion | flops 536870912 | bytes 9961472 | tf_op jit(solution)/shard_map/tas,tws->taw/dot_general | solution.py:32
  249.9 1.8 gather_fusion.9
  251.7 2.8 multiply_reduce_fusion
  254.5 11.9 %psum.109 = f32[512]{0:T(512)S(1)} all-reduce(f32[512]{0:T(512)S(1)} %get-tuple-element.14), channel_id=1, replica_groups=mesh['agent'=8,'res'=4] {'agent'}, use_global_device_ids=true, to_apply=%region_11.12 | all-reduce | flops 512 | bytes 4096 | tf_op jit(solution)/shard_map/psum | solution.py:43
  266.3 0.6 multiply_reduce_fusion.5
  267.6 0.6 fusion
  268.2 9.8 %all-reduce.1 = (f32[]{:T(128)}, f32[]{:T(128)}, f32[]{:T(128)}, f32[]{:T(128)}, f32[]{:T(128)}) all-reduce(f32[]{:T(128)S(6)} %mul.99, f32[]{:T(128)S(6)} %mul.100, f32[]{:T(128)S(6)} %mul.101, f32[]{:T(128)S(6)} %mul.102, f32[]{:T(128)S(6)} %mul.103), channel_id=1, replica_groups=mesh['agent'=8,'res'=4] {'res'}, use_global_device_ids=true, to_apply=%region_13.14 | all-reduce | flops 5 | bytes 40 | tf_op jit(solution)/shard_map/psum | solution.py:48
  281.3 42.5 %all-reduce = (f32[]{:T(128)}, f32[]{:T(128)}, f32[]{:T(128)}, f32[]{:T(128)}, f32[]{:T(128)}) all-reduce(f32[]{:T(128)} %get-tuple-element.13, f32[]{:T(128)} %get-tuple-element.12, f32[]{:T(128)} %get-tuple-element.11, f32[]{:T(128)} %get-tuple-element.10, f32[]{:T(128)} %get-tuple-element.9), channel_id=1, replica_groups=mesh['agent'=8,'res'=4] {'agent','res'}, use_global_device_ids=true, to_apply=%region_23.24 | all-reduce | flops 5 | bytes 40 | tf_op jit(solution)/shard_map/psum | solution.py:44
  327.2 0.6 stack.41
  327.8 0.6 stack.47
  (13 shorter events, 0.0 us)
Async XLA Ops:
  7.2 36.1 %all-gather.6.cloned.1.call-start = ((), (), s32[]{:S(2)}) async-start(), calls=%async_computation | async-start | bytes 1310720 | tf_op jit(solution)/shard_map/all_gather | solution.py:34
  14.0 79.1 %all-gather.8.cloned.1.call-start = ((), (), s32[]{:S(2)}) async-start(), calls=%async_computation.1 | async-start | bytes 1310720 | tf_op jit(solution)/shard_map/all_gather | solution.py:34
  18.1 44.9 %copy-start.1 = (f32[512]{0:T(512)S(1)}, f32[512]{0:T(512)}, u32[]{:S(2)}) copy-start(f32[512]{0:T(512)} %param.10) | copy-start | bytes 6148
  18.1 44.9 %copy-start.3 = (f32[512]{0:T(512)S(1)}, f32[512]{0:T(512)}, u32[]{:S(2)}) copy-start(f32[512]{0:T(512)} %param.11) | copy-start | bytes 6148
  18.1 45.5 %copy-start = (f32[256,512]{1,0:T(8,128)S(1)}, f32[256,512]{1,0:T(8,128)}, u32[]{:S(2)}) copy-start(f32[256,512]{1,0:T(8,128)} %param.6) | copy-start | bytes 1572868
  65.6 77.0 %all-gather.10.cloned.1.call-start = ((), (), s32[]{:S(2)}) async-start(), calls=%async_computation.2 | async-start | bytes 1310720 | tf_op jit(solution)/shard_map/all_gather | solution.py:34
  115.1 77.2 %all-gather.12.cloned.1.call-start = ((), (), s32[]{:S(2)}) async-start(), calls=%async_computation.3 | async-start | bytes 1310720 | tf_op jit(solution)/shard_map/all_gather | solution.py:34
  164.7 78.8 %all-gather.14.cloned.1.call-start = ((), (), s32[]{:S(2)}) async-start(), calls=%async_computation.4 | async-start | bytes 1310720 | tf_op jit(solution)/shard_map/all_gather | solution.py:34
  267.0 61.4 %copy-start.2 = (f32[512]{0:T(512)}, f32[512]{0:T(512)S(1)}, u32[]{:S(2)}) copy-start(f32[512]{0:T(512)S(1)} %get-tuple-element.26) | copy-start | bytes 6148
Sparse Core Ops, SparseCore 0:
  14.2 29.0 all-gather.5
  65.7 27.3 all-gather.7
  115.2 27.3 all-gather.9
  164.8 27.3 all-gather.11
  216.1 27.3 all-gather.13
where the time goes:
time: 336 us; the launch traced here: 335 us
  waiting for transfers between devices  132 us (39%)
  blocking collectives  112 us (33%)
  matrix products  31.9 us (9%)
  between operations  23.8 us (7%)
  local copies, waits for them, and re-layouts  17.4 us (5%)
  other arithmetic  17.3 us (5%)
    all_gather x5, waiting for transfers between devices, on_device(): lax.all_gather(grouped, 'res', axis=2, tiled=True)  132 us
    psum x5, blocking collectives, on_device(): usage_sum = lax.psum(column_sum, 'agent')  59.6 us
    psum x1, blocking collectives, on_device(): dual2 = lax.psum(change_local, ('agent', 'res'))  42.5 us
    dot_general x5, matrix products, on_device(): jnp.einsum('tas,tws->taw', lax.all_gather(grouped, 'res', axis=2, tiled=T...  31.9 us
    psum x1, blocking collectives, on_device(): primal2 = lax.psum(count * jnp.sum((mean_usage - shared) ** 2), 'res')  9.78 us
    gather x5, local copies, waits for them, and re-layouts, on_device(): grouped = rhs[order].reshape(type_count, group_rows, local_width)  9.27 us
  transfers between devices with their start and end apart: 5, of which 5 were waited for; matrix products, arithmetic and copies ran while one was open for 1% of the time, Pallas kernels for 0%

commit v1 on v0

--- a/solution.py
+++ b/solution.py
@@ -40,7 +40,7 @@
         change_local = penalty * penalty * jnp.sum((new_usage - usage) ** 2)
         usage = new_usage
         column_sum = jnp.sum(usage, axis=0)
-        usage_sum = lax.psum(column_sum, "agent")
+        usage_sum = jnp.sum(lax.all_gather(column_sum, "agent"), axis=0)
         dual2 = lax.psum(change_local, ("agent", "res"))
         mean_usage = usage_sum / count
         shared = (cost_weight * target + penalty * (prices + mean_usage)) / (cost_weight + penalty)

time: 336 us -> 319 us (0.949); the launches traced: 335 us -> 314 us
  blocking collectives: 112 us -> 94.6 us
    psum x5 -> x0, blocking collectives: 59.6 us -> none  [on_device(): usage_sum = lax.psum(column_sum, 'agent')]
    all_gather x0 -> x5, blocking collectives: none -> 43.6 us  [on_device(): usage_sum = jnp.sum(lax.all_gather(column_sum, 'agent'), axis=0)]
    all_gather x5, waiting for transfers between devices: 132 us -> 129 us  [on_device(): lax.all_gather(grouped, 'res', axis=2, tiled=True)]
where the time goes in v1:
time: 319 us; the launch traced here: 314 us
  waiting for transfers between devices  129 us (40%)
  blocking collectives  94.6 us (30%)
  matrix products  31.9 us (10%)
  between operations  23.9 us (7%)
  local copies, waits for them, and re-layouts  17.4 us (5%)
  other arithmetic  17.4 us (5%)
    all_gather x5, waiting for transfers between devices, on_device(): lax.all_gather(grouped, 'res', axis=2, tiled=True)  129 us
    all_gather x5, blocking collectives, on_device(): usage_sum = jnp.sum(lax.all_gather(column_sum, 'agent'), axis=0)  43.6 us
    psum x1, blocking collectives, on_device(): dual2 = lax.psum(change_local, ('agent', 'res'))  40.6 us
    dot_general x5, matrix products, on_device(): jnp.einsum('tas,tws->taw', lax.all_gather(grouped, 'res', axis=2, tiled=T...  31.9 us
    psum x1, blocking collectives, on_device(): primal2 = lax.psum(count * jnp.sum((mean_usage - shared) ** 2), 'res')  10.3 us
    gather x5, local copies, waits for them, and re-layouts, on_device(): grouped = rhs[order].reshape(type_count, group_rows, local_width)  9.27 us
    gather x5, local copies, waits for them, and re-layouts, on_device(): new_usage = product.reshape(local_agents, local_width)[restore]  6.45 us
  transfers between devices with their start and end apart: 5, of which 5 were waited for; matrix products, arithmetic and copies ran while one was open for 1% of the time, Pallas kernels for 0%

profile of v1, /device:TPU:12, one launch (start us, length us, event | category | flops | bytes accessed | tf_op | source)
XLA Modules:
  0.0 314.3 jit_solution(1774206657027140786)
XLA Ops:
  7.2 0.0 all-gather.16.cloned.1.call-start
  7.2 3.8 %sort.31 = (s32[256]{0:T(256)}, s32[256]{0:T(256)S(1)}) sort(s32[256]{0:T(256)} %param.7, s32[256]{0:T(256)S(1)} %iota.7), dimensions={0}, to_apply=%region_0.0 | sort | flops 2048 | bytes 4096 | tf_op jit(solution)/shard_map/jit(argsort)/sort | solution.py:18
  11.1 1.1 subtract_convert_fusion.4
  12.2 1.9 gather_fusion
  14.0 0.0 all-gather.16.cloned.1.call-update
  14.0 0.0 all-gather.18.cloned.1.call-start
  14.1 3.2 %sort.32 = (s32[256]{0:T(256)}, s32[256]{0:T(256)S(1)}) sort(s32[256]{0:T(256)S(1)} %get-tuple-element.7, s32[256]{0:T(256)S(1)} %iota.8), dimensions={0}, to_apply=%region_1.2 | sort | flops 2048 | bytes 4096 | tf_op jit(solution)/shard_map/jit(argsort)/sort | solution.py:19
  17.3 0.7 convert_element_type.19
  18.0 0.1 copy.12
  18.1 0.0 copy-start.1
  18.1 0.0 copy-start.3
  18.1 0.0 copy-start
  18.2 25.1 %all-gather.16.cloned.1.call-done = bf16[4,64,2048]{2,1,0:T(8,128)(2,1)} async-done(((bf16[4,64,512]{2,1,0:T(8,128)(2,1)}), bf16[4,64,2048]{2,1,0:T(8,128)(2,1)}) %all-gather.16.cloned.1.call-update) | async-done | bytes 1048592 | tf_op jit(solution)/shard_map/all_gather | solution.py:34
  43.3 6.4 %fusion.13 = f32[4,64,512]{2,1,0:T(8,128)S(1)} fusion(bf16[4,64,2048]{2,1,0:T(8,128)(2,1)} %all-gather.16.cloned.1.call-done, bf16[4,512,2048]{2,1,0:T(8,128)(2,1)} %param.9), kind=kOutput, calls=%fused_computation.56 | convolution fusion | flops 536870912 | bytes 9961472 | tf_op jit(solution)/shard_map/tas,tws->taw/dot_general | solution.py:32
  49.7 1.0 gather_fusion.1
  50.7 0.3 broadcast_in_dim.11
  51.0 0.1 fusion.12
  51.1 8.9 %all-gather.5 = f32[8,1,512]{2,1,0:T(1,128)S(1)} all-gather(f32[1,1,512]{2,1,0:T(1,128)S(1)} %bitcast.63), channel_id=2, replica_groups=mesh['agent'=8,'res'=4] {'agent'}, dimensions={0}, use_global_device_ids=true | all-gather | bytes 18432 | tf_op jit(solution)/shard_map/all_gather | solution.py:43
  60.0 0.0 copy-done.3
  60.0 0.6 multiply_reduce_fusion.9
  60.6 0.1 subtract_convert_fusion.3
  60.8 1.9 gather_fusion.2
  62.6 0.0 all-gather.18.cloned.1.call-update
  62.6 0.0 all-gather.20.cloned.1.call-start
  62.7 26.6 %all-gather.18.cloned.1.call-done = bf16[4,64,2048]{2,1,0:T(8,128)(2,1)} async-done(((bf16[4,64,512]{2,1,0:T(8,128)(2,1)}), bf16[4,64,2048]{2,1,0:T(8,128)(2,1)}) %all-gather.18.cloned.1.call-update) | async-done | bytes 1048592 | tf_op jit(solution)/shard_map/all_gather | solution.py:34
  89.2 6.4 %fusion.14 = f32[4,64,512]{2,1,0:T(8,128)S(1)} fusion(bf16[4,64,2048]{2,1,0:T(8,128)(2,1)} %all-gather.18.cloned.1.call-done, bf16[4,512,2048]{2,1,0:T(8,128)(2,1)} %param.9), kind=kOutput, calls=%fused_computation.57 | convolution fusion | flops 536870912 | bytes 9961472 | tf_op jit(solution)/shard_map/tas,tws->taw/dot_general | solution.py:32
  95.6 1.0 gather_fusion.3
  96.6 0.1 fusion.11
  96.7 8.9 %all-gather.6 = f32[8,1,512]{2,1,0:T(1,128)S(1)} all-gather(f32[1,1,512]{2,1,0:T(1,128)S(1)} %bitcast.64), channel_id=3, replica_groups=mesh['agent'=8,'res'=4] {'agent'}, dimensions={0}, use_global_device_ids=true | all-gather | bytes 18432 | tf_op jit(solution)/shard_map/all_gather | solution.py:43
  105.6 0.6 multiply_reduce_fusion.8
  106.2 0.1 subtract_convert_fusion.2
  106.4 1.9 gather_fusion.4
  108.2 0.0 all-gather.20.cloned.1.call-update
  108.2 0.0 all-gather.22.cloned.1.call-start
  108.3 26.6 %all-gather.20.cloned.1.call-done = bf16[4,64,2048]{2,1,0:T(8,128)(2,1)} async-done(((bf16[4,64,512]{2,1,0:T(8,128)(2,1)}), bf16[4,64,2048]{2,1,0:T(8,128)(2,1)}) %all-gather.20.cloned.1.call-update) | async-done | bytes 1048592 | tf_op jit(solution)/shard_map/all_gather | solution.py:34
  134.8 6.4 %fusion.15 = f32[4,64,512]{2,1,0:T(8,128)S(1)} fusion(bf16[4,64,2048]{2,1,0:T(8,128)(2,1)} %all-gather.20.cloned.1.call-done, bf16[4,512,2048]{2,1,0:T(8,128)(2,1)} %param.9), kind=kOutput, calls=%fused_computation.58 | convolution fusion | flops 536870912 | bytes 9961472 | tf_op jit(solution)/shard_map/tas,tws->taw/dot_general | solution.py:32
  141.2 1.0 gather_fusion.5
  142.2 0.1 fusion.10
  142.3 9.0 %all-gather.7 = f32[8,1,512]{2,1,0:T(1,128)S(1)} all-gather(f32[1,1,512]{2,1,0:T(1,128)S(1)} %bitcast.65), channel_id=4, replica_groups=mesh['agent'=8,'res'=4] {'agent'}, dimensions={0}, use_global_device_ids=true | all-gather | bytes 18432 | tf_op jit(solution)/shard_map/all_gather | solution.py:43
  151.4 0.6 multiply_reduce_fusion.7
  152.0 0.1 subtract_convert_fusion.1
  152.1 1.9 gather_fusion.6
  154.0 0.0 all-gather.22.cloned.1.call-update
  154.0 0.0 all-gather.24.cloned.1.call-start
  154.1 26.6 %all-gather.22.cloned.1.call-done = bf16[4,64,2048]{2,1,0:T(8,128)(2,1)} async-done(((bf16[4,64,512]{2,1,0:T(8,128)(2,1)}), bf16[4,64,2048]{2,1,0:T(8,128)(2,1)}) %all-gather.22.cloned.1.call-update) | async-done | bytes 1048592 | tf_op jit(solution)/shard_map/all_gather | solution.py:34
  180.6 6.4 %fusion.16 = f32[4,64,512]{2,1,0:T(8,128)S(1)} fusion(bf16[4,64,2048]{2,1,0:T(8,128)(2,1)} %all-gather.22.cloned.1.call-done, bf16[4,512,2048]{2,1,0:T(8,128)(2,1)} %param.9), kind=kOutput, calls=%fused_computation.59 | convolution fusion | flops 536870912 | bytes 9961472 | tf_op jit(solution)/shard_map/tas,tws->taw/dot_general | solution.py:32
  187.0 1.8 gather_fusion.7
  188.8 1.2 fusion.9
  189.9 8.9 %all-gather.8 = f32[8,1,512]{2,1,0:T(1,128)S(1)} all-gather(f32[1,1,512]{2,1,0:T(1,128)S(1)} %bitcast.66), channel_id=5, replica_groups=mesh['agent'=8,'res'=4] {'agent'}, dimensions={0}, use_global_device_ids=true | all-gather | bytes 18432 | tf_op jit(solution)/shard_map/all_gather | solution.py:43
  198.8 0.6 multiply_reduce_fusion.6
  199.4 0.1 subtract_convert_fusion
  199.6 1.9 gather_fusion.8
  201.4 0.0 all-gather.24.cloned.1.call-update
  204.0 24.0 %all-gather.24.cloned.1.call-done = bf16[4,64,2048]{2,1,0:T(8,128)(2,1)} async-done(((bf16[4,64,512]{2,1,0:T(8,128)(2,1)}), bf16[4,64,2048]{2,1,0:T(8,128)(2,1)}) %all-gather.24.cloned.1.call-update) | async-done | bytes 1048592 | tf_op jit(solution)/shard_map/all_gather | solution.py:34
  228.0 6.4 %fusion.17 = f32[4,64,512]{2,1,0:T(8,128)S(1)} fusion(bf16[4,64,2048]{2,1,0:T(8,128)(2,1)} %all-gather.24.cloned.1.call-done, bf16[4,512,2048]{2,1,0:T(8,128)(2,1)} %param.9), kind=kOutput, calls=%fused_computation.60 | convolution fusion | flops 536870912 | bytes 9961472 | tf_op jit(solution)/shard_map/tas,tws->taw/dot_general | solution.py:32
  234.4 1.8 gather_fusion.9
  236.2 2.8 multiply_reduce_fusion
  239.0 40.6 %all-reduce = (f32[]{:T(128)}, f32[]{:T(128)}, f32[]{:T(128)}, f32[]{:T(128)}, f32[]{:T(128)}) all-reduce(f32[]{:T(128)} %get-tuple-element.13, f32[]{:T(128)} %get-tuple-element.12, f32[]{:T(128)} %get-tuple-element.11, f32[]{:T(128)} %get-tuple-element.10, f32[]{:T(128)} %get-tuple-element.9), channel_id=1, replica_groups=mesh['agent'=8,'res'=4] {'agent','res'}, use_global_device_ids=true, to_apply=%region_23.24 | all-reduce | flops 5 | bytes 40 | tf_op jit(solution)/shard_map/psum | solution.py:44
  283.0 8.0 %all-gather.9 = f32[8,1,512]{2,1,0:T(1,128)S(1)} all-gather(f32[1,1,512]{2,1,0:T(1,128)S(1)} %bitcast.62), channel_id=6, replica_groups=mesh['agent'=8,'res'=4] {'agent'}, dimensions={0}, use_global_device_ids=true | all-gather | bytes 18432 | tf_op jit(solution)/shard_map/all_gather | solution.py:43
  291.0 0.6 multiply_reduce_fusion.5
  292.2 0.6 fusion
  292.9 10.3 %all-reduce.1 = (f32[]{:T(128)}, f32[]{:T(128)}, f32[]{:T(128)}, f32[]{:T(128)}, f32[]{:T(128)}) all-reduce(f32[]{:T(128)S(6)} %mul.99, f32[]{:T(128)S(6)} %mul.100, f32[]{:T(128)S(6)} %mul.101, f32[]{:T(128)S(6)} %mul.102, f32[]{:T(128)S(6)} %mul.103), channel_id=1, replica_groups=mesh['agent'=8,'res'=4] {'res'}, use_global_device_ids=true, to_apply=%region_13.14 | all-reduce | flops 5 | bytes 40 | tf_op jit(solution)/shard_map/psum | solution.py:48
  306.6 0.6 stack.47
  307.2 0.6 stack.41
  (18 shorter events, 0.2 us)
Async XLA Ops:
  7.2 36.1 %all-gather.16.cloned.1.call-start = ((), (), s32[]{:S(2)}) async-start(), calls=%async_computation | async-start | bytes 1310720 | tf_op jit(solution)/shard_map/all_gather | solution.py:34
  14.0 75.2 %all-gather.18.cloned.1.call-start = ((), (), s32[]{:S(2)}) async-start(), calls=%async_computation.1 | async-start | bytes 1310720 | tf_op jit(solution)/shard_map/all_gather | solution.py:34
  18.1 41.9 %copy-start.1 = (f32[512]{0:T(512)S(1)}, f32[512]{0:T(512)}, u32[]{:S(2)}) copy-start(f32[512]{0:T(512)} %param.10) | copy-start | bytes 6148
  18.1 41.9 %copy-start.3 = (f32[512]{0:T(512)S(1)}, f32[512]{0:T(512)}, u32[]{:S(2)}) copy-start(f32[512]{0:T(512)} %param.11) | copy-start | bytes 6148
  18.1 42.5 %copy-start = (f32[256,512]{1,0:T(8,128)S(1)}, f32[256,512]{1,0:T(8,128)}, u32[]{:S(2)}) copy-start(f32[256,512]{1,0:T(8,128)} %param.6) | copy-start | bytes 1572868
  62.6 72.2 %all-gather.20.cloned.1.call-start = ((), (), s32[]{:S(2)}) async-start(), calls=%async_computation.2 | async-start | bytes 1310720 | tf_op jit(solution)/shard_map/all_gather | solution.py:34
  108.2 72.4 %all-gather.22.cloned.1.call-start = ((), (), s32[]{:S(2)}) async-start(), calls=%async_computation.3 | async-start | bytes 1310720 | tf_op jit(solution)/shard_map/all_gather | solution.py:34
  154.0 74.0 %all-gather.24.cloned.1.call-start = ((), (), s32[]{:S(2)}) async-start(), calls=%async_computation.4 | async-start | bytes 1310720 | tf_op jit(solution)/shard_map/all_gather | solution.py:34
  291.6 16.2 %copy-start.2 = (f32[512]{0:T(512)}, f32[512]{0:T(512)S(1)}, u32[]{:S(2)}) copy-start(f32[512]{0:T(512)S(1)} %get-tuple-element.26) | copy-start | bytes 6148
Sparse Core Ops, SparseCore 0:
  14.2 29.0 all-gather.15
  62.8 26.4 all-gather.17
  108.4 26.4 all-gather.19
  154.1 26.4 all-gather.21
  201.6 26.4 all-gather.23
